TPU v7x, 128 devices: a whole 4x4x4 slice. The times are simulated.
128 devices in a mesh: grp: 16 (over x, y), chan: 8 (over z, core).
Axes of the slice: x: 4, y: 4, z: 4, core: 2. Of those that a mesh axis runs over, the one named last changes fastest.
Arguments:
- spectra: bfloat16 [2048, 2, 2, 8192], P(('grp', 'chan')), may hold values from -45 to 45
- pair_blocks: int32 [16, 8, 18, 2], P('grp', 'chan'), may hold values from 0 to 63
- owners: int32 [16, 8, 18, 1], P('grp', 'chan'), may hold values from 0 to 15; in each aligned block of 18 rows (0 to 17, 18 to 35, ..., all dimensions but the last counted through in order) at most 3 rows name the same one
Outputs:
- stacks: float32 [16, 8, 48, 4, 1024], P('grp', 'chan')
Inputs may be any that keep to these rules, and one draw needn't show every extreme that they name: `owners`: at most 3 of one device's 18 pair blocks name the same owner.
All inputs are finite; a program needn't handle non-finite values.
Results may differ from a plain program's by a relative error of at most 0.011.
Values may be sent and summed in bfloat16 or wider, within the bound.
A program may use at most 128 MiB of HBM per device.

v0:
```python
import jax
import jax.numpy as jnp
from jax import lax
from jax.sharding import PartitionSpec as P

F = 8192
LAGS = 1024
BLK = 2
NB_SRC = 18
MOST = 3
WINDOWS = 2


def table_block(start, count):
    bins = start + jnp.arange(count, dtype=jnp.int32)
    lag_index = jnp.arange(LAGS, dtype=jnp.int32) - LAGS // 2
    phase = bins[:, None] * lag_index[None, :] % (2 * F)
    angle = phase.astype(jnp.float32) * (jnp.pi / F)
    weight = jnp.where(bins == 0, 1.0, 2.0).astype(jnp.float32) / jnp.sqrt(jnp.float32(F))
    cos_part = (jnp.cos(angle) * weight[:, None]).astype(jnp.bfloat16)
    sin_part = (-jnp.sin(angle) * weight[:, None]).astype(jnp.bfloat16)
    return (cos_part, sin_part)


def to_lags(rows):
    width_block = min(512, F)
    real_rows = rows[:, 0]
    imag_rows = rows[:, 1]

    def add_block(turn, total):
        start = (turn * width_block).astype(jnp.int32)
        cos_part, sin_part = table_block(start, width_block)
        real_slice = lax.dynamic_slice_in_dim(real_rows, start, width_block, 1)
        imag_slice = lax.dynamic_slice_in_dim(imag_rows, start, width_block, 1)
        total = total + jnp.dot(real_slice, cos_part, preferred_element_type=jnp.float32)
        return total + jnp.dot(imag_slice, sin_part, preferred_element_type=jnp.float32)

    start_total = jnp.zeros((rows.shape[0], LAGS), jnp.float32)
    return lax.fori_loop(0, F // width_block, add_block, start_total)


def whiten(spectra):
    values = spectra.astype(jnp.float32)
    power = values[:, :, 0] ** 2 + values[:, :, 1] ** 2
    level = jnp.mean(power, axis=-1, keepdims=True) + 1e-05
    scale = lax.rsqrt(power + 0.1 * level)
    return (values * scale[:, :, None, :]).astype(jnp.bfloat16)


def cross_pairs(left, right):
    real_left = left[..., :, None, :, 0, :]
    imag_left = left[..., :, None, :, 1, :]
    real_right = right[..., None, :, :, 0, :]
    imag_right = right[..., None, :, :, 1, :]
    real_part = real_left * real_right + imag_left * imag_right
    imag_part = imag_left * real_right - real_left * imag_right
    both = jnp.stack([real_part, imag_part], axis=-2)
    return both.astype(jnp.bfloat16)


def local(spectra, pair_blocks, owners):
    groups_count = lax.axis_size("grp")
    slot_count = groups_count * MOST
    white = whiten(spectra)
    panel = lax.all_gather(white, "chan", axis=0, tiled=True)
    blocks = pair_blocks[0, 0]
    offsets = jnp.arange(BLK, dtype=jnp.int32)
    left_idx = blocks[:, 0][:, None] * BLK + offsets
    right_idx = blocks[:, 1][:, None] * BLK + offsets
    left = jnp.take(panel, left_idx, axis=0).astype(jnp.float32)
    right = jnp.take(panel, right_idx, axis=0).astype(jnp.float32)
    cross = cross_pairs(left, right).reshape(NB_SRC, BLK * BLK, WINDOWS, 2, F)
    owner_list = owners[0, 0, :, 0]
    same = owner_list[:, None] == owner_list[None, :]
    earlier = jnp.arange(NB_SRC)[None, :] < jnp.arange(NB_SRC)[:, None]
    order_rank = jnp.sum(jnp.logical_and(same, earlier), axis=1)
    slot_ids = owner_list * MOST + order_rank
    chooser = slot_ids[None, :] == jnp.arange(slot_count, dtype=jnp.int32)[:, None]
    pairs = BLK * BLK
    summed = jnp.zeros((groups_count, MOST, pairs, 2, F), jnp.float32)
    for window in range(WINDOWS):
        placed = jnp.einsum(
            "ms,sprf->mprf",
            chooser.astype(jnp.bfloat16),
            cross[:, :, window],
            preferred_element_type=jnp.float32,
        )
        summed = summed + lax.all_to_all(
            placed.astype(jnp.bfloat16).reshape(groups_count, MOST, pairs, 2, F),
            "grp",
            split_axis=0,
            concat_axis=0,
            tiled=True,
        ).astype(jnp.float32)
    received = (summed / WINDOWS).astype(jnp.bfloat16)
    shape_now = received.shape
    rows = received.reshape(-1, 2, F)
    result = to_lags(rows).reshape(shape_now[0], shape_now[1], pairs, LAGS)
    return result.reshape(1, 1, slot_count, pairs, LAGS)


def solution(mesh):
    return jax.shard_map(
        local,
        mesh=mesh,
        in_specs=(
            P(("grp", "chan"), None, None, None),
            P("grp", "chan", None, None),
            P("grp", "chan", None, None),
        ),
        out_specs=P("grp", "chan", None, None, None),
        check_vma=False,
    )
```

profile of v0, /device:TPU:20, one launch (start us, length us, event | category | flops | bytes accessed | tf_op | source)
XLA Modules:
  0.0 685.6 jit_solution(13492980502422854776)
XLA Ops:
  6.5 1.8 copy_convert_fusion
  8.6 0.3 rsqrt_bitcast_fusion
  8.9 0.7 copy-done.3
  9.6 0.6 multiply_convert_fusion.5
  10.2 2.1 copy.50
  13.3 51.4 %all-gather.2.cloned.1.call-done = bf16[128,2,2,8192]{3,2,1,0:T(2,128)(2,1)} async-done(((bf16[16,2,2,8192]{3,2,1,0:T(2,128)(2,1)}), bf16[128,2,2,8192]{3,2,1,0:T(2,128)(2,1)}) %all-gather.2.cloned.1.call-update) | async-done | bytes 8388624 | tf_op jit(solution)/shard_map/all_gather | solution.py:65
  64.7 11.3 %gather_fusion = bf16[36,2,2,8192]{3,2,1,0:T(2,128)(2,1)S(1)} fusion(bf16[128,2,2,8192]{3,2,1,0:T(2,128)(2,1)} %all-gather.2.cloned.1.call-done, s32[1024]{0:T(1024)S(1)} %pad_clamp_fusion.1), kind=kCustom, calls=%fused_computation.clone | custom fusion | bytes 4718736 | tf_op jit(solution)/shard_map/jit(_take)/gather | solution.py:70
  75.9 2.1 fusion.23
  78.1 5.4 fusion.36
  83.5 3.3 copy.81
  86.7 3.3 copy.83
  90.0 11.5 %gather_fusion.1 = bf16[36,2,2,8192]{3,2,1,0:T(2,128)(2,1)S(1)} fusion(bf16[128,2,2,8192]{3,2,1,0:T(2,128)(2,1)} %all-gather.2.cloned.1.call-done, s32[1024]{0:T(1024)S(1)} %pad_clamp_fusion), kind=kCustom, calls=%fused_computation.1.clone | custom fusion | bytes 4718736 | tf_op jit(solution)/shard_map/jit(_take)/gather | solution.py:71
  101.5 2.1 fusion.24
  103.6 5.4 fusion.37
  109.0 1.5 copy.80
  110.6 1.5 copy.82
  112.1 0.4 copy-done.1
  112.5 1.7 add_convert_fusion
  114.2 2.2 convolution_convert_fusion.1
  116.5 11.0 %copy.58 = bf16[48,4,2,8192]{3,2,1,0:T(2,128)(2,1)} copy(bf16[48,4,2,8192]{3,0,2,1:T(8,128)(2,1)S(1)} %convolution_convert_fusion.1) | data formatting | bytes 12582912 | tf_op jit(solution)/shard_map/convert_element_type | solution.py:89
  127.5 7.2 %all-to-all-start = ((bf16[16,3,4,2,8192]{4,3,2,1,0:T(2,128)(2,1)}), bf16[16,3,4,2,8192]{4,3,2,1,0:T(2,128)(2,1)}, u32[]{:S(2)}, u32[]{:S(2)}) async-start(bf16[16,3,4,2,8192]{4,3,2,1,0:T(2,128)(2,1)} %bitcast.52), calls=%async_computation | async-start | bytes 12582912 | tf_op jit(solution)/shard_map/all_to_all | solution.py:88
  134.7 3.3 convolution_convert_fusion
  138.0 11.0 %copy.59 = bf16[48,4,2,8192]{3,2,1,0:T(2,128)(2,1)} copy(bf16[48,4,2,8192]{3,0,2,1:T(8,128)(2,1)S(1)} %convolution_convert_fusion) | data formatting | bytes 12582912 | tf_op jit(solution)/shard_map/convert_element_type | solution.py:89
  149.0 89.4 %all-to-all-done = bf16[16,3,4,2,8192]{4,3,2,1,0:T(2,128)(2,1)} async-done(((bf16[16,3,4,2,8192]{4,3,2,1,0:T(2,128)(2,1)}), bf16[16,3,4,2,8192]{4,3,2,1,0:T(2,128)(2,1)}, u32[]{:S(2)}, u32[]{:S(2)}) %all-to-all-start) | async-done | bytes 6291488 | tf_op jit(solution)/shard_map/all_to_all | solution.py:88
  238.5 14.3 %all-to-all-start.1 = ((bf16[16,3,4,2,8192]{4,3,2,1,0:T(2,128)(2,1)}), bf16[16,3,4,2,8192]{4,3,2,1,0:T(2,128)(2,1)}, u32[]{:S(2)}, u32[]{:S(2)}) async-start(bf16[16,3,4,2,8192]{4,3,2,1,0:T(2,128)(2,1)} %bitcast.51), calls=%async_computation.1 | async-start | bytes 12582912 | tf_op jit(solution)/shard_map/all_to_all | solution.py:88
  252.8 99.9 %all-to-all-done.1 = bf16[16,3,4,2,8192]{4,3,2,1,0:T(2,128)(2,1)} async-done(((bf16[16,3,4,2,8192]{4,3,2,1,0:T(2,128)(2,1)}), bf16[16,3,4,2,8192]{4,3,2,1,0:T(2,128)(2,1)}, u32[]{:S(2)}, u32[]{:S(2)}) %all-to-all-start.1) | async-done | bytes 6291488 | tf_op jit(solution)/shard_map/all_to_all | solution.py:88
  352.7 11.2 %multiply_convert_fusion.4 = bf16[16,3,4,2,8192]{4,3,2,1,0:T(2,128)(2,1)S(1)} fusion(bf16[16,3,4,2,8192]{4,3,2,1,0:T(2,128)(2,1)} %all-to-all-done.1, bf16[16,3,4,2,8192]{4,3,2,1,0:T(2,128)(2,1)} %all-to-all-done), kind=kLoop, calls=%fused_computation.29 | loop fusion | flops 15728640 | bytes 18874368 | tf_op jit(solution)/shard_map/convert_element_type | solution.py:95
  363.9 13.4 %fusion.35 = (bf16[192,1,8192]{2,1,0:T(2,128)(2,1)S(1)}, bf16[192,1,8192]{2,1,0:T(2,128)(2,1)S(1)}) fusion(bf16[192,2,8192]{2,1,0:T(2,128)(2,1)S(1)} %bitcast.46), kind=kLoop, calls=%fused_computation.77 | loop fusion | bytes 12582912 | tf_op jit(solution)/shard_map/slice | solution.py:28
  377.3 3.4 copy.78
  380.8 5.1 copy.79
  385.9 290.4 %while.16 = (s32[]{:T(128)}, f32[192,1024]{1,0:T(8,128)}, bf16[192,8192]{1,0:T(8,128)(2,1)}, bf16[192,8192]{1,0:T(8,128)(2,1)S(1)}, s32[]{:T(128)}, /*index=5*/s32[]{:T(128)}, s32[]{:T(128)}, s32[]{:T(128)}) while((s32[]{:T(128)}, f32[192,1024]{1,0:T(8,128)}, bf16[192,8192]{1,0:T(8,128)(2,1)}, bf16[192,8192]{1,0:T(8,128)(2,1)S(1)}, ...), condition=%wide.region_3.5_spmd.clone, body=%wide.region_2.4_spmd.clone.sunk | while | flops 420548096 | bytes 3563677 | solution.py:39
  386.1 8.9 %convolution_add_fusion.4 = f32[192,1024]{1,0:T(8,128)S(1)} fusion(f32[512]{0:T(512)S(1)} %select_multiply_fusion.2, s32[1024]{0:T(1024)S(1)} %iota_add_fusion.4, s32[512]{0:T(512)S(1)} %iota_add_fusion.5, f32[192,1024]{1,0:T(8,128)} %get-tuple-element.190, pred[]{:T(512)S(6)} %compare.4, bf16[192,8192]{1,0:T(8,128)(2,1)} %get-tuple-element.199, ...), kind=kOutput, calls=%fused_computation.13.clone.1 | convolution fusion | flops 210108416 | bytes 1777669 | tf_op jit(solution)/shard_map/while/body/eval_jaxpr/dot_general | solution.py:35
  395.0 9.0 %convolution_add_fusion.5 = f32[192,1024]{1,0:T(8,128)} fusion(f32[192,1024]{1,0:T(8,128)S(1)} %convolution_add_fusion.4, f32[512]{0:T(512)S(1)} %select_multiply_fusion.2, s32[1024]{0:T(1024)S(1)} %iota_add_fusion.4, s32[512]{0:T(512)S(1)} %iota_add_fusion.5, bf16[192,8192]{1,0:T(8,128)(2,1)S(1)} %get-tuple-element.200, s32[]{:T(128)S(6)} %select_n.93), kind=kOutput, calls=%fused_computation.12.clone.1 | convolution fusion | flops 210436096 | bytes 1777668 | tf_op jit(solution)/shard_map/while/body/eval_jaxpr/dot_general | solution.py:36
  403.9 9.2 %convolution_add_fusion.4 = f32[192,1024]{1,0:T(8,128)S(1)} fusion(f32[512]{0:T(512)S(1)} %select_multiply_fusion.2, s32[1024]{0:T(1024)S(1)} %iota_add_fusion.4, s32[512]{0:T(512)S(1)} %iota_add_fusion.5, f32[192,1024]{1,0:T(8,128)} %get-tuple-element.190, pred[]{:T(512)S(6)} %compare.4, bf16[192,8192]{1,0:T(8,128)(2,1)} %get-tuple-element.199, ...), kind=kOutput, calls=%fused_computation.13.clone.1 | convolution fusion | flops 210108416 | bytes 1777669 | tf_op jit(solution)/shard_map/while/body/eval_jaxpr/dot_general | solution.py:35
  413.1 9.0 %convolution_add_fusion.5 = f32[192,1024]{1,0:T(8,128)} fusion(f32[192,1024]{1,0:T(8,128)S(1)} %convolution_add_fusion.4, f32[512]{0:T(512)S(1)} %select_multiply_fusion.2, s32[1024]{0:T(1024)S(1)} %iota_add_fusion.4, s32[512]{0:T(512)S(1)} %iota_add_fusion.5, bf16[192,8192]{1,0:T(8,128)(2,1)S(1)} %get-tuple-element.200, s32[]{:T(128)S(6)} %select_n.93), kind=kOutput, calls=%fused_computation.12.clone.1 | convolution fusion | flops 210436096 | bytes 1777668 | tf_op jit(solution)/shard_map/while/body/eval_jaxpr/dot_general | solution.py:36
  422.1 9.2 %convolution_add_fusion.4 = f32[192,1024]{1,0:T(8,128)S(1)} fusion(f32[512]{0:T(512)S(1)} %select_multiply_fusion.2, s32[1024]{0:T(1024)S(1)} %iota_add_fusion.4, s32[512]{0:T(512)S(1)} %iota_add_fusion.5, f32[192,1024]{1,0:T(8,128)} %get-tuple-element.190, pred[]{:T(512)S(6)} %compare.4, bf16[192,8192]{1,0:T(8,128)(2,1)} %get-tuple-element.199, ...), kind=kOutput, calls=%fused_computation.13.clone.1 | convolution fusion | flops 210108416 | bytes 1777669 | tf_op jit(solution)/shard_map/while/body/eval_jaxpr/dot_general | solution.py:35
  431.3 9.0 %convolution_add_fusion.5 = f32[192,1024]{1,0:T(8,128)} fusion(f32[192,1024]{1,0:T(8,128)S(1)} %convolution_add_fusion.4, f32[512]{0:T(512)S(1)} %select_multiply_fusion.2, s32[1024]{0:T(1024)S(1)} %iota_add_fusion.4, s32[512]{0:T(512)S(1)} %iota_add_fusion.5, bf16[192,8192]{1,0:T(8,128)(2,1)S(1)} %get-tuple-element.200, s32[]{:T(128)S(6)} %select_n.93), kind=kOutput, calls=%fused_computation.12.clone.1 | convolution fusion | flops 210436096 | bytes 1777668 | tf_op jit(solution)/shard_map/while/body/eval_jaxpr/dot_general | solution.py:36
  440.2 9.2 %convolution_add_fusion.4 = f32[192,1024]{1,0:T(8,128)S(1)} fusion(f32[512]{0:T(512)S(1)} %select_multiply_fusion.2, s32[1024]{0:T(1024)S(1)} %iota_add_fusion.4, s32[512]{0:T(512)S(1)} %iota_add_fusion.5, f32[192,1024]{1,0:T(8,128)} %get-tuple-element.190, pred[]{:T(512)S(6)} %compare.4, bf16[192,8192]{1,0:T(8,128)(2,1)} %get-tuple-element.199, ...), kind=kOutput, calls=%fused_computation.13.clone.1 | convolution fusion | flops 210108416 | bytes 1777669 | tf_op jit(solution)/shard_map/while/body/eval_jaxpr/dot_general | solution.py:35
  449.4 9.0 %convolution_add_fusion.5 = f32[192,1024]{1,0:T(8,128)} fusion(f32[192,1024]{1,0:T(8,128)S(1)} %convolution_add_fusion.4, f32[512]{0:T(512)S(1)} %select_multiply_fusion.2, s32[1024]{0:T(1024)S(1)} %iota_add_fusion.4, s32[512]{0:T(512)S(1)} %iota_add_fusion.5, bf16[192,8192]{1,0:T(8,128)(2,1)S(1)} %get-tuple-element.200, s32[]{:T(128)S(6)} %select_n.93), kind=kOutput, calls=%fused_computation.12.clone.1 | convolution fusion | flops 210436096 | bytes 1777668 | tf_op jit(solution)/shard_map/while/body/eval_jaxpr/dot_general | solution.py:36
  458.4 9.2 %convolution_add_fusion.4 = f32[192,1024]{1,0:T(8,128)S(1)} fusion(f32[512]{0:T(512)S(1)} %select_multiply_fusion.2, s32[1024]{0:T(1024)S(1)} %iota_add_fusion.4, s32[512]{0:T(512)S(1)} %iota_add_fusion.5, f32[192,1024]{1,0:T(8,128)} %get-tuple-element.190, pred[]{:T(512)S(6)} %compare.4, bf16[192,8192]{1,0:T(8,128)(2,1)} %get-tuple-element.199, ...), kind=kOutput, calls=%fused_computation.13.clone.1 | convolution fusion | flops 210108416 | bytes 1777669 | tf_op jit(solution)/shard_map/while/body/eval_jaxpr/dot_general | solution.py:35
  467.6 9.0 %convolution_add_fusion.5 = f32[192,1024]{1,0:T(8,128)} fusion(f32[192,1024]{1,0:T(8,128)S(1)} %convolution_add_fusion.4, f32[512]{0:T(512)S(1)} %select_multiply_fusion.2, s32[1024]{0:T(1024)S(1)} %iota_add_fusion.4, s32[512]{0:T(512)S(1)} %iota_add_fusion.5, bf16[192,8192]{1,0:T(8,128)(2,1)S(1)} %get-tuple-element.200, s32[]{:T(128)S(6)} %select_n.93), kind=kOutput, calls=%fused_computation.12.clone.1 | convolution fusion | flops 210436096 | bytes 1777668 | tf_op jit(solution)/shard_map/while/body/eval_jaxpr/dot_general | solution.py:36
  476.6 9.2 %convolution_add_fusion.4 = f32[192,1024]{1,0:T(8,128)S(1)} fusion(f32[512]{0:T(512)S(1)} %select_multiply_fusion.2, s32[1024]{0:T(1024)S(1)} %iota_add_fusion.4, s32[512]{0:T(512)S(1)} %iota_add_fusion.5, f32[192,1024]{1,0:T(8,128)} %get-tuple-element.190, pred[]{:T(512)S(6)} %compare.4, bf16[192,8192]{1,0:T(8,128)(2,1)} %get-tuple-element.199, ...), kind=kOutput, calls=%fused_computation.13.clone.1 | convolution fusion | flops 210108416 | bytes 1777669 | tf_op jit(solution)/shard_map/while/body/eval_jaxpr/dot_general | solution.py:35
  485.7 9.0 %convolution_add_fusion.5 = f32[192,1024]{1,0:T(8,128)} fusion(f32[192,1024]{1,0:T(8,128)S(1)} %convolution_add_fusion.4, f32[512]{0:T(512)S(1)} %select_multiply_fusion.2, s32[1024]{0:T(1024)S(1)} %iota_add_fusion.4, s32[512]{0:T(512)S(1)} %iota_add_fusion.5, bf16[192,8192]{1,0:T(8,128)(2,1)S(1)} %get-tuple-element.200, s32[]{:T(128)S(6)} %select_n.93), kind=kOutput, calls=%fused_computation.12.clone.1 | convolution fusion | flops 210436096 | bytes 1777668 | tf_op jit(solution)/shard_map/while/body/eval_jaxpr/dot_general | solution.py:36
  494.7 9.2 %convolution_add_fusion.4 = f32[192,1024]{1,0:T(8,128)S(1)} fusion(f32[512]{0:T(512)S(1)} %select_multiply_fusion.2, s32[1024]{0:T(1024)S(1)} %iota_add_fusion.4, s32[512]{0:T(512)S(1)} %iota_add_fusion.5, f32[192,1024]{1,0:T(8,128)} %get-tuple-element.190, pred[]{:T(512)S(6)} %compare.4, bf16[192,8192]{1,0:T(8,128)(2,1)} %get-tuple-element.199, ...), kind=kOutput, calls=%fused_computation.13.clone.1 | convolution fusion | flops 210108416 | bytes 1777669 | tf_op jit(solution)/shard_map/while/body/eval_jaxpr/dot_general | solution.py:35
  503.9 9.0 %convolution_add_fusion.5 = f32[192,1024]{1,0:T(8,128)} fusion(f32[192,1024]{1,0:T(8,128)S(1)} %convolution_add_fusion.4, f32[512]{0:T(512)S(1)} %select_multiply_fusion.2, s32[1024]{0:T(1024)S(1)} %iota_add_fusion.4, s32[512]{0:T(512)S(1)} %iota_add_fusion.5, bf16[192,8192]{1,0:T(8,128)(2,1)S(1)} %get-tuple-element.200, s32[]{:T(128)S(6)} %select_n.93), kind=kOutput, calls=%fused_computation.12.clone.1 | convolution fusion | flops 210436096 | bytes 1777668 | tf_op jit(solution)/shard_map/while/body/eval_jaxpr/dot_general | solution.py:36
  512.9 9.2 %convolution_add_fusion.4 = f32[192,1024]{1,0:T(8,128)S(1)} fusion(f32[512]{0:T(512)S(1)} %select_multiply_fusion.2, s32[1024]{0:T(1024)S(1)} %iota_add_fusion.4, s32[512]{0:T(512)S(1)} %iota_add_fusion.5, f32[192,1024]{1,0:T(8,128)} %get-tuple-element.190, pred[]{:T(512)S(6)} %compare.4, bf16[192,8192]{1,0:T(8,128)(2,1)} %get-tuple-element.199, ...), kind=kOutput, calls=%fused_computation.13.clone.1 | convolution fusion | flops 210108416 | bytes 1777669 | tf_op jit(solution)/shard_map/while/body/eval_jaxpr/dot_general | solution.py:35
  522.1 9.0 %convolution_add_fusion.5 = f32[192,1024]{1,0:T(8,128)} fusion(f32[192,1024]{1,0:T(8,128)S(1)} %convolution_add_fusion.4, f32[512]{0:T(512)S(1)} %select_multiply_fusion.2, s32[1024]{0:T(1024)S(1)} %iota_add_fusion.4, s32[512]{0:T(512)S(1)} %iota_add_fusion.5, bf16[192,8192]{1,0:T(8,128)(2,1)S(1)} %get-tuple-element.200, s32[]{:T(128)S(6)} %select_n.93), kind=kOutput, calls=%fused_computation.12.clone.1 | convolution fusion | flops 210436096 | bytes 1777668 | tf_op jit(solution)/shard_map/while/body/eval_jaxpr/dot_general | solution.py:36
  531.0 9.2 %convolution_add_fusion.4 = f32[192,1024]{1,0:T(8,128)S(1)} fusion(f32[512]{0:T(512)S(1)} %select_multiply_fusion.2, s32[1024]{0:T(1024)S(1)} %iota_add_fusion.4, s32[512]{0:T(512)S(1)} %iota_add_fusion.5, f32[192,1024]{1,0:T(8,128)} %get-tuple-element.190, pred[]{:T(512)S(6)} %compare.4, bf16[192,8192]{1,0:T(8,128)(2,1)} %get-tuple-element.199, ...), kind=kOutput, calls=%fused_computation.13.clone.1 | convolution fusion | flops 210108416 | bytes 1777669 | tf_op jit(solution)/shard_map/while/body/eval_jaxpr/dot_general | solution.py:35
  540.2 9.0 %convolution_add_fusion.5 = f32[192,1024]{1,0:T(8,128)} fusion(f32[192,1024]{1,0:T(8,128)S(1)} %convolution_add_fusion.4, f32[512]{0:T(512)S(1)} %select_multiply_fusion.2, s32[1024]{0:T(1024)S(1)} %iota_add_fusion.4, s32[512]{0:T(512)S(1)} %iota_add_fusion.5, bf16[192,8192]{1,0:T(8,128)(2,1)S(1)} %get-tuple-element.200, s32[]{:T(128)S(6)} %select_n.93), kind=kOutput, calls=%fused_computation.12.clone.1 | convolution fusion | flops 210436096 | bytes 1777668 | tf_op jit(solution)/shard_map/while/body/eval_jaxpr/dot_general | solution.py:36
  549.2 9.2 %convolution_add_fusion.4 = f32[192,1024]{1,0:T(8,128)S(1)} fusion(f32[512]{0:T(512)S(1)} %select_multiply_fusion.2, s32[1024]{0:T(1024)S(1)} %iota_add_fusion.4, s32[512]{0:T(512)S(1)} %iota_add_fusion.5, f32[192,1024]{1,0:T(8,128)} %get-tuple-element.190, pred[]{:T(512)S(6)} %compare.4, bf16[192,8192]{1,0:T(8,128)(2,1)} %get-tuple-element.199, ...), kind=kOutput, calls=%fused_computation.13.clone.1 | convolution fusion | flops 210108416 | bytes 1777669 | tf_op jit(solution)/shard_map/while/body/eval_jaxpr/dot_general | solution.py:35
  558.4 9.0 %convolution_add_fusion.5 = f32[192,1024]{1,0:T(8,128)} fusion(f32[192,1024]{1,0:T(8,128)S(1)} %convolution_add_fusion.4, f32[512]{0:T(512)S(1)} %select_multiply_fusion.2, s32[1024]{0:T(1024)S(1)} %iota_add_fusion.4, s32[512]{0:T(512)S(1)} %iota_add_fusion.5, bf16[192,8192]{1,0:T(8,128)(2,1)S(1)} %get-tuple-element.200, s32[]{:T(128)S(6)} %select_n.93), kind=kOutput, calls=%fused_computation.12.clone.1 | convolution fusion | flops 210436096 | bytes 1777668 | tf_op jit(solution)/shard_map/while/body/eval_jaxpr/dot_general | solution.py:36
  567.3 9.2 %convolution_add_fusion.4 = f32[192,1024]{1,0:T(8,128)S(1)} fusion(f32[512]{0:T(512)S(1)} %select_multiply_fusion.2, s32[1024]{0:T(1024)S(1)} %iota_add_fusion.4, s32[512]{0:T(512)S(1)} %iota_add_fusion.5, f32[192,1024]{1,0:T(8,128)} %get-tuple-element.190, pred[]{:T(512)S(6)} %compare.4, bf16[192,8192]{1,0:T(8,128)(2,1)} %get-tuple-element.199, ...), kind=kOutput, calls=%fused_computation.13.clone.1 | convolution fusion | flops 210108416 | bytes 1777669 | tf_op jit(solution)/shard_map/while/body/eval_jaxpr/dot_general | solution.py:35
  576.5 9.0 %convolution_add_fusion.5 = f32[192,1024]{1,0:T(8,128)} fusion(f32[192,1024]{1,0:T(8,128)S(1)} %convolution_add_fusion.4, f32[512]{0:T(512)S(1)} %select_multiply_fusion.2, s32[1024]{0:T(1024)S(1)} %iota_add_fusion.4, s32[512]{0:T(512)S(1)} %iota_add_fusion.5, bf16[192,8192]{1,0:T(8,128)(2,1)S(1)} %get-tuple-element.200, s32[]{:T(128)S(6)} %select_n.93), kind=kOutput, calls=%fused_computation.12.clone.1 | convolution fusion | flops 210436096 | bytes 1777668 | tf_op jit(solution)/shard_map/while/body/eval_jaxpr/dot_general | solution.py:36
  585.5 9.2 %convolution_add_fusion.4 = f32[192,1024]{1,0:T(8,128)S(1)} fusion(f32[512]{0:T(512)S(1)} %select_multiply_fusion.2, s32[1024]{0:T(1024)S(1)} %iota_add_fusion.4, s32[512]{0:T(512)S(1)} %iota_add_fusion.5, f32[192,1024]{1,0:T(8,128)} %get-tuple-element.190, pred[]{:T(512)S(6)} %compare.4, bf16[192,8192]{1,0:T(8,128)(2,1)} %get-tuple-element.199, ...), kind=kOutput, calls=%fused_computation.13.clone.1 | convolution fusion | flops 210108416 | bytes 1777669 | tf_op jit(solution)/shard_map/while/body/eval_jaxpr/dot_general | solution.py:35
  594.7 9.0 %convolution_add_fusion.5 = f32[192,1024]{1,0:T(8,128)} fusion(f32[192,1024]{1,0:T(8,128)S(1)} %convolution_add_fusion.4, f32[512]{0:T(512)S(1)} %select_multiply_fusion.2, s32[1024]{0:T(1024)S(1)} %iota_add_fusion.4, s32[512]{0:T(512)S(1)} %iota_add_fusion.5, bf16[192,8192]{1,0:T(8,128)(2,1)S(1)} %get-tuple-element.200, s32[]{:T(128)S(6)} %select_n.93), kind=kOutput, calls=%fused_computation.12.clone.1 | convolution fusion | flops 210436096 | bytes 1777668 | tf_op jit(solution)/shard_map/while/body/eval_jaxpr/dot_general | solution.py:36
  603.6 9.2 %convolution_add_fusion.4 = f32[192,1024]{1,0:T(8,128)S(1)} fusion(f32[512]{0:T(512)S(1)} %select_multiply_fusion.2, s32[1024]{0:T(1024)S(1)} %iota_add_fusion.4, s32[512]{0:T(512)S(1)} %iota_add_fusion.5, f32[192,1024]{1,0:T(8,128)} %get-tuple-element.190, pred[]{:T(512)S(6)} %compare.4, bf16[192,8192]{1,0:T(8,128)(2,1)} %get-tuple-element.199, ...), kind=kOutput, calls=%fused_computation.13.clone.1 | convolution fusion | flops 210108416 | bytes 1777669 | tf_op jit(solution)/shard_map/while/body/eval_jaxpr/dot_general | solution.py:35
  612.8 9.0 %convolution_add_fusion.5 = f32[192,1024]{1,0:T(8,128)} fusion(f32[192,1024]{1,0:T(8,128)S(1)} %convolution_add_fusion.4, f32[512]{0:T(512)S(1)} %select_multiply_fusion.2, s32[1024]{0:T(1024)S(1)} %iota_add_fusion.4, s32[512]{0:T(512)S(1)} %iota_add_fusion.5, bf16[192,8192]{1,0:T(8,128)(2,1)S(1)} %get-tuple-element.200, s32[]{:T(128)S(6)} %select_n.93), kind=kOutput, calls=%fused_computation.12.clone.1 | convolution fusion | flops 210436096 | bytes 1777668 | tf_op jit(solution)/shard_map/while/body/eval_jaxpr/dot_general | solution.py:36
  621.8 9.2 %convolution_add_fusion.4 = f32[192,1024]{1,0:T(8,128)S(1)} fusion(f32[512]{0:T(512)S(1)} %select_multiply_fusion.2, s32[1024]{0:T(1024)S(1)} %iota_add_fusion.4, s32[512]{0:T(512)S(1)} %iota_add_fusion.5, f32[192,1024]{1,0:T(8,128)} %get-tuple-element.190, pred[]{:T(512)S(6)} %compare.4, bf16[192,8192]{1,0:T(8,128)(2,1)} %get-tuple-element.199, ...), kind=kOutput, calls=%fused_computation.13.clone.1 | convolution fusion | flops 210108416 | bytes 1777669 | tf_op jit(solution)/shard_map/while/body/eval_jaxpr/dot_general | solution.py:35
  631.0 9.0 %convolution_add_fusion.5 = f32[192,1024]{1,0:T(8,128)} fusion(f32[192,1024]{1,0:T(8,128)S(1)} %convolution_add_fusion.4, f32[512]{0:T(512)S(1)} %select_multiply_fusion.2, s32[1024]{0:T(1024)S(1)} %iota_add_fusion.4, s32[512]{0:T(512)S(1)} %iota_add_fusion.5, bf16[192,8192]{1,0:T(8,128)(2,1)S(1)} %get-tuple-element.200, s32[]{:T(128)S(6)} %select_n.93), kind=kOutput, calls=%fused_computation.12.clone.1 | convolution fusion | flops 210436096 | bytes 1777668 | tf_op jit(solution)/shard_map/while/body/eval_jaxpr/dot_general | solution.py:36
  640.0 9.2 %convolution_add_fusion.4 = f32[192,1024]{1,0:T(8,128)S(1)} fusion(f32[512]{0:T(512)S(1)} %select_multiply_fusion.2, s32[1024]{0:T(1024)S(1)} %iota_add_fusion.4, s32[512]{0:T(512)S(1)} %iota_add_fusion.5, f32[192,1024]{1,0:T(8,128)} %get-tuple-element.190, pred[]{:T(512)S(6)} %compare.4, bf16[192,8192]{1,0:T(8,128)(2,1)} %get-tuple-element.199, ...), kind=kOutput, calls=%fused_computation.13.clone.1 | convolution fusion | flops 210108416 | bytes 1777669 | tf_op jit(solution)/shard_map/while/body/eval_jaxpr/dot_general | solution.py:35
  649.1 9.0 %convolution_add_fusion.5 = f32[192,1024]{1,0:T(8,128)} fusion(f32[192,1024]{1,0:T(8,128)S(1)} %convolution_add_fusion.4, f32[512]{0:T(512)S(1)} %select_multiply_fusion.2, s32[1024]{0:T(1024)S(1)} %iota_add_fusion.4, s32[512]{0:T(512)S(1)} %iota_add_fusion.5, bf16[192,8192]{1,0:T(8,128)(2,1)S(1)} %get-tuple-element.200, s32[]{:T(128)S(6)} %select_n.93), kind=kOutput, calls=%fused_computation.12.clone.1 | convolution fusion | flops 210436096 | bytes 1777668 | tf_op jit(solution)/shard_map/while/body/eval_jaxpr/dot_general | solution.py:36
  658.1 9.2 %convolution_add_fusion.4 = f32[192,1024]{1,0:T(8,128)S(1)} fusion(f32[512]{0:T(512)S(1)} %select_multiply_fusion.2, s32[1024]{0:T(1024)S(1)} %iota_add_fusion.4, s32[512]{0:T(512)S(1)} %iota_add_fusion.5, f32[192,1024]{1,0:T(8,128)} %get-tuple-element.190, pred[]{:T(512)S(6)} %compare.4, bf16[192,8192]{1,0:T(8,128)(2,1)} %get-tuple-element.199, ...), kind=kOutput, calls=%fused_computation.13.clone.1 | convolution fusion | flops 210108416 | bytes 1777669 | tf_op jit(solution)/shard_map/while/body/eval_jaxpr/dot_general | solution.py:35
  667.3 9.0 %convolution_add_fusion.5 = f32[192,1024]{1,0:T(8,128)} fusion(f32[192,1024]{1,0:T(8,128)S(1)} %convolution_add_fusion.4, f32[512]{0:T(512)S(1)} %select_multiply_fusion.2, s32[1024]{0:T(1024)S(1)} %iota_add_fusion.4, s32[512]{0:T(512)S(1)} %iota_add_fusion.5, bf16[192,8192]{1,0:T(8,128)(2,1)S(1)} %get-tuple-element.200, s32[]{:T(128)S(6)} %select_n.93), kind=kOutput, calls=%fused_computation.12.clone.1 | convolution fusion | flops 210436096 | bytes 1777668 | tf_op jit(solution)/shard_map/while/body/eval_jaxpr/dot_general | solution.py:36
  676.3 2.2 reshape_reshape.3
  (76 shorter events, 1.3 us)
Async XLA Ops:
  6.5 58.1 %all-gather.2.cloned.1.call-start = ((), (), s32[]{:S(2)}) async-start(), calls=%async_computation.2 | async-start | bytes 9437184 | tf_op jit(solution)/shard_map/all_gather | solution.py:65
  8.4 1.2 copy-start.3
  9.6 2.8 copy-start.4
  9.6 3.5 copy-start.5
  109.0 3.1 copy-start.2
  110.6 2.0 copy-start.1
  114.2 2.2 copy-start
  127.5 111.0 %all-to-all-start = ((bf16[16,3,4,2,8192]{4,3,2,1,0:T(2,128)(2,1)}), bf16[16,3,4,2,8192]{4,3,2,1,0:T(2,128)(2,1)}, u32[]{:S(2)}, u32[]{:S(2)}) async-start(bf16[16,3,4,2,8192]{4,3,2,1,0:T(2,128)(2,1)} %bitcast.52), calls=%async_computation | async-start | bytes 12582912 | tf_op jit(solution)/shard_map/all_to_all | solution.py:88
  238.5 114.2 %all-to-all-start.1 = ((bf16[16,3,4,2,8192]{4,3,2,1,0:T(2,128)(2,1)}), bf16[16,3,4,2,8192]{4,3,2,1,0:T(2,128)(2,1)}, u32[]{:S(2)}, u32[]{:S(2)}) async-start(bf16[16,3,4,2,8192]{4,3,2,1,0:T(2,128)(2,1)} %bitcast.51), calls=%async_computation.1 | async-start | bytes 12582912 | tf_op jit(solution)/shard_map/all_to_all | solution.py:88
Sparse Core Ops, SparseCore 0:
  12.5 52.0 all-gather.1
where the time goes:
time: 689 us; the launch traced here: 686 us
  matrix products  295 us (43%)
  waiting for transfers between devices  241 us (35%)
  local copies, waits for them, and re-layouts  93.2 us (14%)
  starting transfers between devices  21.5 us (3%)
  other arithmetic  20.5 us (3%)
  between operations  13.8 us (2%)
    all_to_all x2, waiting for transfers between devices, local(): lax.all_to_all(placed.astype(jnp.bfloat16).reshape(groups_count, MOST, pa...  189 us
    dot_general x16, matrix products, add_block(): jnp.dot(real_slice, cos_part, preferred_element_type=jnp.float32)  146 us
    dot_general x16, matrix products, add_block(): jnp.dot(imag_slice, sin_part, preferred_element_type=jnp.float32)  143 us
    all_gather x1, waiting for transfers between devices, local(): panel = lax.all_gather(white, 'chan', axis=0, tiled=True)  51.4 us
    convert_element_type x2, local copies, waits for them, and re-layouts, local(): placed.astype(jnp.bfloat16).reshape(groups_count, MOST, pairs, 2, F)  22 us
    all_to_all x2, starting transfers between devices, local(): lax.all_to_all(placed.astype(jnp.bfloat16).reshape(groups_count, MOST, pa...  21.5 us
  transfers between devices with their start and end apart: 3, of which 3 were waited for; matrix products, arithmetic and copies ran while one was open for 2% of the time, Pallas kernels for 0%

commit v1 on v0

--- a/solution.py
+++ b/solution.py
@@ -9,6 +9,19 @@
 NB_SRC = 18
 MOST = 3
 WINDOWS = 2
+
+
+def collect(x, axis, dim):
+    ways = lax.axis_size(axis)
+    up = [(d, (d + 1) % ways) for d in range(ways)]
+    down = [(d, (d - 1) % ways) for d in range(ways)]
+    earlier, later = ([x], [x])
+    for _ in range(ways // 2):
+        earlier.append(lax.ppermute(earlier[-1], axis, up))
+    for _ in range((ways - 1) // 2):
+        later.append(lax.ppermute(later[-1], axis, down))
+    line = jnp.concatenate([*earlier[::-1], *later[1:]], axis=dim)
+    return jnp.roll(line, (lax.axis_index(axis) - ways // 2) * x.shape[dim], axis=dim)
 
 
 def table_block(start, count):
@@ -62,7 +75,7 @@
     groups_count = lax.axis_size("grp")
     slot_count = groups_count * MOST
     white = whiten(spectra)
-    panel = lax.all_gather(white, "chan", axis=0, tiled=True)
+    panel = collect(white, "chan", 0)
     blocks = pair_blocks[0, 0]
     offsets = jnp.arange(BLK, dtype=jnp.int32)
     left_idx = blocks[:, 0][:, None] * BLK + offsets

time: 689 us -> 738 us (1.071)
  the two profiles are of different devices: /device:TPU:20 before, /device:TPU:124 now
where the time goes in v1:
time: 738 us; the launch traced here: 730 us
  matrix products  295 us (40%)
  waiting for transfers between devices  243 us (33%)
  local copies, waits for them, and re-layouts  140 us (19%)
  starting transfers between devices  27.1 us (4%)
  other arithmetic  23.5 us (3%)
    all_to_all x2, waiting for transfers between devices, local(): lax.all_to_all(placed.astype(jnp.bfloat16).reshape(groups_count, MOST, pa...  192 us
    dot_general x16, matrix products, add_block(): jnp.dot(real_slice, cos_part, preferred_element_type=jnp.float32)  146 us
    dot_general x16, matrix products, add_block(): jnp.dot(imag_slice, sin_part, preferred_element_type=jnp.float32)  143 us
    ppermute x4, waiting for transfers between devices, collect(): earlier.append(lax.ppermute(earlier[-1], axis, up))  51.2 us
    unnamed x31, local copies, waits for them, and re-layouts  33.8 us
    dynamic_slice x2, local copies, waits for them, and re-layouts, collect(): jnp.roll(line, (lax.axis_index(axis) - ways // 2) * x.shape[dim], axis=dim)  23.9 us
    convert_element_type x2, local copies, waits for them, and re-layouts, local(): placed.astype(jnp.bfloat16).reshape(groups_count, MOST, pairs, 2, F)  22 us
    all_to_all x2, starting transfers between devices, local(): lax.all_to_all(placed.astype(jnp.bfloat16).reshape(groups_count, MOST, pa...  21.9 us
  transfers between devices with their start and end apart: 9, of which 6 were waited for; matrix products, arithmetic and copies ran while one was open for 4% of the time, Pallas kernels for 0%

profile of v1, /device:TPU:124, one launch (start us, length us, event | category | flops | bytes accessed | tf_op | source)
XLA Modules:
  0.0 730.4 jit_solution(1469261591629827362)
XLA Ops:
  3.7 14.2 %collective-permute-done = bf16[16,2,2,8192]{3,0,2,1:T(8,128)(2,1)S(1)} collective-permute-done((bf16[16,2,2,8192]{3,0,2,1:T(8,128)(2,1)S(1)}, bf16[16,2,2,8192]{3,0,2,1:T(8,128)(2,1)S(1)}, u32[]{:S(2)}, u32[]{:S(2)}) %collective-permute-start) | collective-permute-done | bytes 1048608 | tf_op jit(solution)/shard_map/ppermute | solution.py:20
  19.7 12.5 %collective-permute-done.1 = bf16[16,2,2,8192]{3,0,2,1:T(8,128)(2,1)S(1)} collective-permute-done((bf16[16,2,2,8192]{3,0,2,1:T(8,128)(2,1)S(1)}, bf16[16,2,2,8192]{3,0,2,1:T(8,128)(2,1)S(1)}, u32[]{:S(2)}, u32[]{:S(2)}) %collective-permute-start.1) | collective-permute-done | bytes 1048608 | tf_op jit(solution)/shard_map/ppermute | solution.py:20
  34.9 12.6 %collective-permute-done.2 = bf16[16,2,2,8192]{3,0,2,1:T(8,128)(2,1)} collective-permute-done((bf16[16,2,2,8192]{3,0,2,1:T(8,128)(2,1)S(1)}, bf16[16,2,2,8192]{3,0,2,1:T(8,128)(2,1)}, u32[]{:S(2)}, u32[]{:S(2)}) %collective-permute-start.2) | collective-permute-done | bytes 1048608 | tf_op jit(solution)/shard_map/ppermute | solution.py:20
  50.1 11.9 %collective-permute-done.3 = bf16[16,2,2,8192]{3,0,2,1:T(8,128)(2,1)} collective-permute-done((bf16[16,2,2,8192]{3,0,2,1:T(8,128)(2,1)}, bf16[16,2,2,8192]{3,0,2,1:T(8,128)(2,1)}, u32[]{:S(2)}, u32[]{:S(2)}) %collective-permute-start.3) | collective-permute-done | bytes 1048608 | tf_op jit(solution)/shard_map/ppermute | solution.py:20
  62.0 2.3 constant_dynamic-update-slice_fusion.15
  64.3 2.2 constant_dynamic-update-slice_fusion.14
  70.1 2.2 constant_dynamic-update-slice_fusion.10
  75.6 2.2 constant_dynamic-update-slice_fusion.7
  77.9 2.3 constant_dynamic-update-slice_fusion.6
  83.7 2.2 constant_dynamic-update-slice_fusion.2
  85.9 2.3 constant_dynamic-update-slice_fusion.1
  89.3 7.6 %constant_dynamic-slice_fusion = bf16[128,2,2,8192]{3,0,2,1:T(8,128)(2,1)} fusion(bf16[256,2,2,8192]{3,0,2,1:T(8,128)(2,1)} %constant_dynamic-update-slice_fusion, s32[]{:T(128)S(6)} %select_n.66), kind=kLoop, calls=%fused_computation.91 | loop fusion | bytes 16777220 | tf_op jit(solution)/shard_map/jit(_roll_dynamic)/dynamic_slice | solution.py:24
  96.9 16.3 %copy.41 = bf16[128,2,2,8192]{3,2,1,0:T(2,128)(2,1)} copy(bf16[128,2,2,8192]{3,0,2,1:T(8,128)(2,1)} %constant_dynamic-slice_fusion) | data formatting | bytes 16777216 | tf_op jit(solution)/shard_map/jit(_roll_dynamic)/dynamic_slice | solution.py:24
  113.2 11.3 %gather_fusion = bf16[36,2,2,8192]{3,2,1,0:T(2,128)(2,1)S(1)} fusion(bf16[128,2,2,8192]{3,2,1,0:T(2,128)(2,1)} %copy.41, s32[1024]{0:T(1024)S(1)} %pad_clamp_fusion.1), kind=kCustom, calls=%fused_computation.clone | custom fusion | bytes 4718736 | tf_op jit(solution)/shard_map/jit(_take)/gather | solution.py:83
  126.6 5.4 fusion.36
  132.0 3.2 copy.76
  135.3 3.3 copy.78
  138.6 11.5 %gather_fusion.1 = bf16[36,2,2,8192]{3,2,1,0:T(2,128)(2,1)S(1)} fusion(bf16[128,2,2,8192]{3,2,1,0:T(2,128)(2,1)} %copy.41, s32[1024]{0:T(1024)S(1)} %pad_clamp_fusion), kind=kCustom, calls=%fused_computation.1.clone | custom fusion | bytes 4718736 | tf_op jit(solution)/shard_map/jit(_take)/gather | solution.py:84
  152.2 5.4 fusion.37
  164.9 11.0 %copy.49 = bf16[48,4,2,8192]{3,2,1,0:T(2,128)(2,1)} copy(bf16[48,4,2,8192]{3,0,2,1:T(8,128)(2,1)S(1)} %convolution_convert_fusion.1) | data formatting | bytes 12582912 | tf_op jit(solution)/shard_map/convert_element_type | solution.py:102
  175.9 7.1 all-to-all-start
  183.0 3.3 convolution_convert_fusion
  186.3 11.0 %copy.50 = bf16[48,4,2,8192]{3,2,1,0:T(2,128)(2,1)} copy(bf16[48,4,2,8192]{3,0,2,1:T(8,128)(2,1)S(1)} %convolution_convert_fusion) | data formatting | bytes 12582912 | tf_op jit(solution)/shard_map/convert_element_type | solution.py:102
  197.3 86.1 %all-to-all-done = bf16[16,3,4,2,8192]{4,3,2,1,0:T(2,128)(2,1)} async-done(((bf16[16,3,4,2,8192]{4,3,2,1,0:T(2,128)(2,1)}), bf16[16,3,4,2,8192]{4,3,2,1,0:T(2,128)(2,1)}, u32[]{:S(2)}, u32[]{:S(2)}) %all-to-all-start) | async-done | bytes 6291488 | tf_op jit(solution)/shard_map/all_to_all | solution.py:101
  283.5 14.8 %all-to-all-start.1 = ((bf16[16,3,4,2,8192]{4,3,2,1,0:T(2,128)(2,1)}), bf16[16,3,4,2,8192]{4,3,2,1,0:T(2,128)(2,1)}, u32[]{:S(2)}, u32[]{:S(2)}) async-start(bf16[16,3,4,2,8192]{4,3,2,1,0:T(2,128)(2,1)} %bitcast.51), calls=%async_computation.1 | async-start | bytes 12582912 | tf_op jit(solution)/shard_map/all_to_all | solution.py:101
  298.2 106.0 %all-to-all-done.1 = bf16[16,3,4,2,8192]{4,3,2,1,0:T(2,128)(2,1)} async-done(((bf16[16,3,4,2,8192]{4,3,2,1,0:T(2,128)(2,1)}), bf16[16,3,4,2,8192]{4,3,2,1,0:T(2,128)(2,1)}, u32[]{:S(2)}, u32[]{:S(2)}) %all-to-all-start.1) | async-done | bytes 6291488 | tf_op jit(solution)/shard_map/all_to_all | solution.py:101
  404.3 11.2 %multiply_convert_fusion.4 = bf16[16,3,4,2,8192]{4,3,2,1,0:T(2,128)(2,1)S(1)} fusion(bf16[16,3,4,2,8192]{4,3,2,1,0:T(2,128)(2,1)} %all-to-all-done.1, bf16[16,3,4,2,8192]{4,3,2,1,0:T(2,128)(2,1)} %all-to-all-done), kind=kLoop, calls=%fused_computation.29 | loop fusion | flops 15728640 | bytes 18874368 | tf_op jit(solution)/shard_map/convert_element_type | solution.py:108
  415.4 13.4 %fusion.35 = (bf16[192,1,8192]{2,1,0:T(2,128)(2,1)S(1)}, bf16[192,1,8192]{2,1,0:T(2,128)(2,1)S(1)}) fusion(bf16[192,2,8192]{2,1,0:T(2,128)(2,1)S(1)} %bitcast.46), kind=kLoop, calls=%fused_computation.94 | loop fusion | bytes 12582912 | tf_op jit(solution)/shard_map/slice | solution.py:41
  428.9 3.4 copy.73
  432.3 5.1 copy.74
  437.4 290.3 %while.16 = (s32[]{:T(128)}, f32[192,1024]{1,0:T(8,128)}, bf16[192,8192]{1,0:T(8,128)(2,1)}, bf16[192,8192]{1,0:T(8,128)(2,1)S(1)}, s32[]{:T(128)}, /*index=5*/s32[]{:T(128)}, s32[]{:T(128)}, s32[]{:T(128)}) while((s32[]{:T(128)}, f32[192,1024]{1,0:T(8,128)}, bf16[192,8192]{1,0:T(8,128)(2,1)}, bf16[192,8192]{1,0:T(8,128)(2,1)S(1)}, ...), condition=%wide.region_3.5_spmd.clone, body=%wide.region_2.4_spmd.clone.sunk | while | flops 420548096 | bytes 3563677 | solution.py:52
  437.7 8.9 %convolution_add_fusion.4 = f32[192,1024]{1,0:T(8,128)S(1)} fusion(f32[512]{0:T(512)S(1)} %select_multiply_fusion.2, s32[1024]{0:T(1024)S(1)} %iota_add_fusion.4, s32[512]{0:T(512)S(1)} %iota_add_fusion.5, f32[192,1024]{1,0:T(8,128)} %get-tuple-element.190, pred[]{:T(512)S(6)} %compare.5, bf16[192,8192]{1,0:T(8,128)(2,1)} %get-tuple-element.199, ...), kind=kOutput, calls=%fused_computation.13.clone.1 | convolution fusion | flops 210108416 | bytes 1777669 | tf_op jit(solution)/shard_map/while/body/eval_jaxpr/dot_general | solution.py:48
  446.5 9.0 %convolution_add_fusion.5 = f32[192,1024]{1,0:T(8,128)} fusion(f32[192,1024]{1,0:T(8,128)S(1)} %convolution_add_fusion.4, f32[512]{0:T(512)S(1)} %select_multiply_fusion.2, s32[1024]{0:T(1024)S(1)} %iota_add_fusion.4, s32[512]{0:T(512)S(1)} %iota_add_fusion.5, bf16[192,8192]{1,0:T(8,128)(2,1)S(1)} %get-tuple-element.200, s32[]{:T(128)S(6)} %select_n.107), kind=kOutput, calls=%fused_computation.12.clone.1 | convolution fusion | flops 210436096 | bytes 1777668 | tf_op jit(solution)/shard_map/while/body/eval_jaxpr/dot_general | solution.py:49
  455.5 9.2 %convolution_add_fusion.4 = f32[192,1024]{1,0:T(8,128)S(1)} fusion(f32[512]{0:T(512)S(1)} %select_multiply_fusion.2, s32[1024]{0:T(1024)S(1)} %iota_add_fusion.4, s32[512]{0:T(512)S(1)} %iota_add_fusion.5, f32[192,1024]{1,0:T(8,128)} %get-tuple-element.190, pred[]{:T(512)S(6)} %compare.5, bf16[192,8192]{1,0:T(8,128)(2,1)} %get-tuple-element.199, ...), kind=kOutput, calls=%fused_computation.13.clone.1 | convolution fusion | flops 210108416 | bytes 1777669 | tf_op jit(solution)/shard_map/while/body/eval_jaxpr/dot_general | solution.py:48
  464.7 9.0 %convolution_add_fusion.5 = f32[192,1024]{1,0:T(8,128)} fusion(f32[192,1024]{1,0:T(8,128)S(1)} %convolution_add_fusion.4, f32[512]{0:T(512)S(1)} %select_multiply_fusion.2, s32[1024]{0:T(1024)S(1)} %iota_add_fusion.4, s32[512]{0:T(512)S(1)} %iota_add_fusion.5, bf16[192,8192]{1,0:T(8,128)(2,1)S(1)} %get-tuple-element.200, s32[]{:T(128)S(6)} %select_n.107), kind=kOutput, calls=%fused_computation.12.clone.1 | convolution fusion | flops 210436096 | bytes 1777668 | tf_op jit(solution)/shard_map/while/body/eval_jaxpr/dot_general | solution.py:49
  473.6 9.2 %convolution_add_fusion.4 = f32[192,1024]{1,0:T(8,128)S(1)} fusion(f32[512]{0:T(512)S(1)} %select_multiply_fusion.2, s32[1024]{0:T(1024)S(1)} %iota_add_fusion.4, s32[512]{0:T(512)S(1)} %iota_add_fusion.5, f32[192,1024]{1,0:T(8,128)} %get-tuple-element.190, pred[]{:T(512)S(6)} %compare.5, bf16[192,8192]{1,0:T(8,128)(2,1)} %get-tuple-element.199, ...), kind=kOutput, calls=%fused_computation.13.clone.1 | convolution fusion | flops 210108416 | bytes 1777669 | tf_op jit(solution)/shard_map/while/body/eval_jaxpr/dot_general | solution.py:48
  482.8 9.0 %convolution_add_fusion.5 = f32[192,1024]{1,0:T(8,128)} fusion(f32[192,1024]{1,0:T(8,128)S(1)} %convolution_add_fusion.4, f32[512]{0:T(512)S(1)} %select_multiply_fusion.2, s32[1024]{0:T(1024)S(1)} %iota_add_fusion.4, s32[512]{0:T(512)S(1)} %iota_add_fusion.5, bf16[192,8192]{1,0:T(8,128)(2,1)S(1)} %get-tuple-element.200, s32[]{:T(128)S(6)} %select_n.107), kind=kOutput, calls=%fused_computation.12.clone.1 | convolution fusion | flops 210436096 | bytes 1777668 | tf_op jit(solution)/shard_map/while/body/eval_jaxpr/dot_general | solution.py:49
  491.8 9.2 %convolution_add_fusion.4 = f32[192,1024]{1,0:T(8,128)S(1)} fusion(f32[512]{0:T(512)S(1)} %select_multiply_fusion.2, s32[1024]{0:T(1024)S(1)} %iota_add_fusion.4, s32[512]{0:T(512)S(1)} %iota_add_fusion.5, f32[192,1024]{1,0:T(8,128)} %get-tuple-element.190, pred[]{:T(512)S(6)} %compare.5, bf16[192,8192]{1,0:T(8,128)(2,1)} %get-tuple-element.199, ...), kind=kOutput, calls=%fused_computation.13.clone.1 | convolution fusion | flops 210108416 | bytes 1777669 | tf_op jit(solution)/shard_map/while/body/eval_jaxpr/dot_general | solution.py:48
  501.0 9.0 %convolution_add_fusion.5 = f32[192,1024]{1,0:T(8,128)} fusion(f32[192,1024]{1,0:T(8,128)S(1)} %convolution_add_fusion.4, f32[512]{0:T(512)S(1)} %select_multiply_fusion.2, s32[1024]{0:T(1024)S(1)} %iota_add_fusion.4, s32[512]{0:T(512)S(1)} %iota_add_fusion.5, bf16[192,8192]{1,0:T(8,128)(2,1)S(1)} %get-tuple-element.200, s32[]{:T(128)S(6)} %select_n.107), kind=kOutput, calls=%fused_computation.12.clone.1 | convolution fusion | flops 210436096 | bytes 1777668 | tf_op jit(solution)/shard_map/while/body/eval_jaxpr/dot_general | solution.py:49
  510.0 9.2 %convolution_add_fusion.4 = f32[192,1024]{1,0:T(8,128)S(1)} fusion(f32[512]{0:T(512)S(1)} %select_multiply_fusion.2, s32[1024]{0:T(1024)S(1)} %iota_add_fusion.4, s32[512]{0:T(512)S(1)} %iota_add_fusion.5, f32[192,1024]{1,0:T(8,128)} %get-tuple-element.190, pred[]{:T(512)S(6)} %compare.5, bf16[192,8192]{1,0:T(8,128)(2,1)} %get-tuple-element.199, ...), kind=kOutput, calls=%fused_computation.13.clone.1 | convolution fusion | flops 210108416 | bytes 1777669 | tf_op jit(solution)/shard_map/while/body/eval_jaxpr/dot_general | solution.py:48
  519.1 9.0 %convolution_add_fusion.5 = f32[192,1024]{1,0:T(8,128)} fusion(f32[192,1024]{1,0:T(8,128)S(1)} %convolution_add_fusion.4, f32[512]{0:T(512)S(1)} %select_multiply_fusion.2, s32[1024]{0:T(1024)S(1)} %iota_add_fusion.4, s32[512]{0:T(512)S(1)} %iota_add_fusion.5, bf16[192,8192]{1,0:T(8,128)(2,1)S(1)} %get-tuple-element.200, s32[]{:T(128)S(6)} %select_n.107), kind=kOutput, calls=%fused_computation.12.clone.1 | convolution fusion | flops 210436096 | bytes 1777668 | tf_op jit(solution)/shard_map/while/body/eval_jaxpr/dot_general | solution.py:49
  528.1 9.2 %convolution_add_fusion.4 = f32[192,1024]{1,0:T(8,128)S(1)} fusion(f32[512]{0:T(512)S(1)} %select_multiply_fusion.2, s32[1024]{0:T(1024)S(1)} %iota_add_fusion.4, s32[512]{0:T(512)S(1)} %iota_add_fusion.5, f32[192,1024]{1,0:T(8,128)} %get-tuple-element.190, pred[]{:T(512)S(6)} %compare.5, bf16[192,8192]{1,0:T(8,128)(2,1)} %get-tuple-element.199, ...), kind=kOutput, calls=%fused_computation.13.clone.1 | convolution fusion | flops 210108416 | bytes 1777669 | tf_op jit(solution)/shard_map/while/body/eval_jaxpr/dot_general | solution.py:48
  537.3 9.0 %convolution_add_fusion.5 = f32[192,1024]{1,0:T(8,128)} fusion(f32[192,1024]{1,0:T(8,128)S(1)} %convolution_add_fusion.4, f32[512]{0:T(512)S(1)} %select_multiply_fusion.2, s32[1024]{0:T(1024)S(1)} %iota_add_fusion.4, s32[512]{0:T(512)S(1)} %iota_add_fusion.5, bf16[192,8192]{1,0:T(8,128)(2,1)S(1)} %get-tuple-element.200, s32[]{:T(128)S(6)} %select_n.107), kind=kOutput, calls=%fused_computation.12.clone.1 | convolution fusion | flops 210436096 | bytes 1777668 | tf_op jit(solution)/shard_map/while/body/eval_jaxpr/dot_general | solution.py:49
  546.3 9.2 %convolution_add_fusion.4 = f32[192,1024]{1,0:T(8,128)S(1)} fusion(f32[512]{0:T(512)S(1)} %select_multiply_fusion.2, s32[1024]{0:T(1024)S(1)} %iota_add_fusion.4, s32[512]{0:T(512)S(1)} %iota_add_fusion.5, f32[192,1024]{1,0:T(8,128)} %get-tuple-element.190, pred[]{:T(512)S(6)} %compare.5, bf16[192,8192]{1,0:T(8,128)(2,1)} %get-tuple-element.199, ...), kind=kOutput, calls=%fused_computation.13.clone.1 | convolution fusion | flops 210108416 | bytes 1777669 | tf_op jit(solution)/shard_map/while/body/eval_jaxpr/dot_general | solution.py:48
  555.4 9.0 %convolution_add_fusion.5 = f32[192,1024]{1,0:T(8,128)} fusion(f32[192,1024]{1,0:T(8,128)S(1)} %convolution_add_fusion.4, f32[512]{0:T(512)S(1)} %select_multiply_fusion.2, s32[1024]{0:T(1024)S(1)} %iota_add_fusion.4, s32[512]{0:T(512)S(1)} %iota_add_fusion.5, bf16[192,8192]{1,0:T(8,128)(2,1)S(1)} %get-tuple-element.200, s32[]{:T(128)S(6)} %select_n.107), kind=kOutput, calls=%fused_computation.12.clone.1 | convolution fusion | flops 210436096 | bytes 1777668 | tf_op jit(solution)/shard_map/while/body/eval_jaxpr/dot_general | solution.py:49
  564.4 9.2 %convolution_add_fusion.4 = f32[192,1024]{1,0:T(8,128)S(1)} fusion(f32[512]{0:T(512)S(1)} %select_multiply_fusion.2, s32[1024]{0:T(1024)S(1)} %iota_add_fusion.4, s32[512]{0:T(512)S(1)} %iota_add_fusion.5, f32[192,1024]{1,0:T(8,128)} %get-tuple-element.190, pred[]{:T(512)S(6)} %compare.5, bf16[192,8192]{1,0:T(8,128)(2,1)} %get-tuple-element.199, ...), kind=kOutput, calls=%fused_computation.13.clone.1 | convolution fusion | flops 210108416 | bytes 1777669 | tf_op jit(solution)/shard_map/while/body/eval_jaxpr/dot_general | solution.py:48
  573.6 9.0 %convolution_add_fusion.5 = f32[192,1024]{1,0:T(8,128)} fusion(f32[192,1024]{1,0:T(8,128)S(1)} %convolution_add_fusion.4, f32[512]{0:T(512)S(1)} %select_multiply_fusion.2, s32[1024]{0:T(1024)S(1)} %iota_add_fusion.4, s32[512]{0:T(512)S(1)} %iota_add_fusion.5, bf16[192,8192]{1,0:T(8,128)(2,1)S(1)} %get-tuple-element.200, s32[]{:T(128)S(6)} %select_n.107), kind=kOutput, calls=%fused_computation.12.clone.1 | convolution fusion | flops 210436096 | bytes 1777668 | tf_op jit(solution)/shard_map/while/body/eval_jaxpr/dot_general | solution.py:49
  582.6 9.2 %convolution_add_fusion.4 = f32[192,1024]{1,0:T(8,128)S(1)} fusion(f32[512]{0:T(512)S(1)} %select_multiply_fusion.2, s32[1024]{0:T(1024)S(1)} %iota_add_fusion.4, s32[512]{0:T(512)S(1)} %iota_add_fusion.5, f32[192,1024]{1,0:T(8,128)} %get-tuple-element.190, pred[]{:T(512)S(6)} %compare.5, bf16[192,8192]{1,0:T(8,128)(2,1)} %get-tuple-element.199, ...), kind=kOutput, calls=%fused_computation.13.clone.1 | convolution fusion | flops 210108416 | bytes 1777669 | tf_op jit(solution)/shard_map/while/body/eval_jaxpr/dot_general | solution.py:48
  591.7 9.0 %convolution_add_fusion.5 = f32[192,1024]{1,0:T(8,128)} fusion(f32[192,1024]{1,0:T(8,128)S(1)} %convolution_add_fusion.4, f32[512]{0:T(512)S(1)} %select_multiply_fusion.2, s32[1024]{0:T(1024)S(1)} %iota_add_fusion.4, s32[512]{0:T(512)S(1)} %iota_add_fusion.5, bf16[192,8192]{1,0:T(8,128)(2,1)S(1)} %get-tuple-element.200, s32[]{:T(128)S(6)} %select_n.107), kind=kOutput, calls=%fused_computation.12.clone.1 | convolution fusion | flops 210436096 | bytes 1777668 | tf_op jit(solution)/shard_map/while/body/eval_jaxpr/dot_general | solution.py:49
  600.7 9.2 %convolution_add_fusion.4 = f32[192,1024]{1,0:T(8,128)S(1)} fusion(f32[512]{0:T(512)S(1)} %select_multiply_fusion.2, s32[1024]{0:T(1024)S(1)} %iota_add_fusion.4, s32[512]{0:T(512)S(1)} %iota_add_fusion.5, f32[192,1024]{1,0:T(8,128)} %get-tuple-element.190, pred[]{:T(512)S(6)} %compare.5, bf16[192,8192]{1,0:T(8,128)(2,1)} %get-tuple-element.199, ...), kind=kOutput, calls=%fused_computation.13.clone.1 | convolution fusion | flops 210108416 | bytes 1777669 | tf_op jit(solution)/shard_map/while/body/eval_jaxpr/dot_general | solution.py:48
  609.9 9.0 %convolution_add_fusion.5 = f32[192,1024]{1,0:T(8,128)} fusion(f32[192,1024]{1,0:T(8,128)S(1)} %convolution_add_fusion.4, f32[512]{0:T(512)S(1)} %select_multiply_fusion.2, s32[1024]{0:T(1024)S(1)} %iota_add_fusion.4, s32[512]{0:T(512)S(1)} %iota_add_fusion.5, bf16[192,8192]{1,0:T(8,128)(2,1)S(1)} %get-tuple-element.200, s32[]{:T(128)S(6)} %select_n.107), kind=kOutput, calls=%fused_computation.12.clone.1 | convolution fusion | flops 210436096 | bytes 1777668 | tf_op jit(solution)/shard_map/while/body/eval_jaxpr/dot_general | solution.py:49
  618.9 9.2 %convolution_add_fusion.4 = f32[192,1024]{1,0:T(8,128)S(1)} fusion(f32[512]{0:T(512)S(1)} %select_multiply_fusion.2, s32[1024]{0:T(1024)S(1)} %iota_add_fusion.4, s32[512]{0:T(512)S(1)} %iota_add_fusion.5, f32[192,1024]{1,0:T(8,128)} %get-tuple-element.190, pred[]{:T(512)S(6)} %compare.5, bf16[192,8192]{1,0:T(8,128)(2,1)} %get-tuple-element.199, ...), kind=kOutput, calls=%fused_computation.13.clone.1 | convolution fusion | flops 210108416 | bytes 1777669 | tf_op jit(solution)/shard_map/while/body/eval_jaxpr/dot_general | solution.py:48
  628.0 9.0 %convolution_add_fusion.5 = f32[192,1024]{1,0:T(8,128)} fusion(f32[192,1024]{1,0:T(8,128)S(1)} %convolution_add_fusion.4, f32[512]{0:T(512)S(1)} %select_multiply_fusion.2, s32[1024]{0:T(1024)S(1)} %iota_add_fusion.4, s32[512]{0:T(512)S(1)} %iota_add_fusion.5, bf16[192,8192]{1,0:T(8,128)(2,1)S(1)} %get-tuple-element.200, s32[]{:T(128)S(6)} %select_n.107), kind=kOutput, calls=%fused_computation.12.clone.1 | convolution fusion | flops 210436096 | bytes 1777668 | tf_op jit(solution)/shard_map/while/body/eval_jaxpr/dot_general | solution.py:49
  637.0 9.2 %convolution_add_fusion.4 = f32[192,1024]{1,0:T(8,128)S(1)} fusion(f32[512]{0:T(512)S(1)} %select_multiply_fusion.2, s32[1024]{0:T(1024)S(1)} %iota_add_fusion.4, s32[512]{0:T(512)S(1)} %iota_add_fusion.5, f32[192,1024]{1,0:T(8,128)} %get-tuple-element.190, pred[]{:T(512)S(6)} %compare.5, bf16[192,8192]{1,0:T(8,128)(2,1)} %get-tuple-element.199, ...), kind=kOutput, calls=%fused_computation.13.clone.1 | convolution fusion | flops 210108416 | bytes 1777669 | tf_op jit(solution)/shard_map/while/body/eval_jaxpr/dot_general | solution.py:48
  646.2 9.0 %convolution_add_fusion.5 = f32[192,1024]{1,0:T(8,128)} fusion(f32[192,1024]{1,0:T(8,128)S(1)} %convolution_add_fusion.4, f32[512]{0:T(512)S(1)} %select_multiply_fusion.2, s32[1024]{0:T(1024)S(1)} %iota_add_fusion.4, s32[512]{0:T(512)S(1)} %iota_add_fusion.5, bf16[192,8192]{1,0:T(8,128)(2,1)S(1)} %get-tuple-element.200, s32[]{:T(128)S(6)} %select_n.107), kind=kOutput, calls=%fused_computation.12.clone.1 | convolution fusion | flops 210436096 | bytes 1777668 | tf_op jit(solution)/shard_map/while/body/eval_jaxpr/dot_general | solution.py:49
  655.2 9.2 %convolution_add_fusion.4 = f32[192,1024]{1,0:T(8,128)S(1)} fusion(f32[512]{0:T(512)S(1)} %select_multiply_fusion.2, s32[1024]{0:T(1024)S(1)} %iota_add_fusion.4, s32[512]{0:T(512)S(1)} %iota_add_fusion.5, f32[192,1024]{1,0:T(8,128)} %get-tuple-element.190, pred[]{:T(512)S(6)} %compare.5, bf16[192,8192]{1,0:T(8,128)(2,1)} %get-tuple-element.199, ...), kind=kOutput, calls=%fused_computation.13.clone.1 | convolution fusion | flops 210108416 | bytes 1777669 | tf_op jit(solution)/shard_map/while/body/eval_jaxpr/dot_general | solution.py:48
  664.3 9.0 %convolution_add_fusion.5 = f32[192,1024]{1,0:T(8,128)} fusion(f32[192,1024]{1,0:T(8,128)S(1)} %convolution_add_fusion.4, f32[512]{0:T(512)S(1)} %select_multiply_fusion.2, s32[1024]{0:T(1024)S(1)} %iota_add_fusion.4, s32[512]{0:T(512)S(1)} %iota_add_fusion.5, bf16[192,8192]{1,0:T(8,128)(2,1)S(1)} %get-tuple-element.200, s32[]{:T(128)S(6)} %select_n.107), kind=kOutput, calls=%fused_computation.12.clone.1 | convolution fusion | flops 210436096 | bytes 1777668 | tf_op jit(solution)/shard_map/while/body/eval_jaxpr/dot_general | solution.py:49
  673.3 9.2 %convolution_add_fusion.4 = f32[192,1024]{1,0:T(8,128)S(1)} fusion(f32[512]{0:T(512)S(1)} %select_multiply_fusion.2, s32[1024]{0:T(1024)S(1)} %iota_add_fusion.4, s32[512]{0:T(512)S(1)} %iota_add_fusion.5, f32[192,1024]{1,0:T(8,128)} %get-tuple-element.190, pred[]{:T(512)S(6)} %compare.5, bf16[192,8192]{1,0:T(8,128)(2,1)} %get-tuple-element.199, ...), kind=kOutput, calls=%fused_computation.13.clone.1 | convolution fusion | flops 210108416 | bytes 1777669 | tf_op jit(solution)/shard_map/while/body/eval_jaxpr/dot_general | solution.py:48
  682.5 9.0 %convolution_add_fusion.5 = f32[192,1024]{1,0:T(8,128)} fusion(f32[192,1024]{1,0:T(8,128)S(1)} %convolution_add_fusion.4, f32[512]{0:T(512)S(1)} %select_multiply_fusion.2, s32[1024]{0:T(1024)S(1)} %iota_add_fusion.4, s32[512]{0:T(512)S(1)} %iota_add_fusion.5, bf16[192,8192]{1,0:T(8,128)(2,1)S(1)} %get-tuple-element.200, s32[]{:T(128)S(6)} %select_n.107), kind=kOutput, calls=%fused_computation.12.clone.1 | convolution fusion | flops 210436096 | bytes 1777668 | tf_op jit(solution)/shard_map/while/body/eval_jaxpr/dot_general | solution.py:49
  691.5 9.2 %convolution_add_fusion.4 = f32[192,1024]{1,0:T(8,128)S(1)} fusion(f32[512]{0:T(512)S(1)} %select_multiply_fusion.2, s32[1024]{0:T(1024)S(1)} %iota_add_fusion.4, s32[512]{0:T(512)S(1)} %iota_add_fusion.5, f32[192,1024]{1,0:T(8,128)} %get-tuple-element.190, pred[]{:T(512)S(6)} %compare.5, bf16[192,8192]{1,0:T(8,128)(2,1)} %get-tuple-element.199, ...), kind=kOutput, calls=%fused_computation.13.clone.1 | convolution fusion | flops 210108416 | bytes 1777669 | tf_op jit(solution)/shard_map/while/body/eval_jaxpr/dot_general | solution.py:48
  700.6 9.0 %convolution_add_fusion.5 = f32[192,1024]{1,0:T(8,128)} fusion(f32[192,1024]{1,0:T(8,128)S(1)} %convolution_add_fusion.4, f32[512]{0:T(512)S(1)} %select_multiply_fusion.2, s32[1024]{0:T(1024)S(1)} %iota_add_fusion.4, s32[512]{0:T(512)S(1)} %iota_add_fusion.5, bf16[192,8192]{1,0:T(8,128)(2,1)S(1)} %get-tuple-element.200, s32[]{:T(128)S(6)} %select_n.107), kind=kOutput, calls=%fused_computation.12.clone.1 | convolution fusion | flops 210436096 | bytes 1777668 | tf_op jit(solution)/shard_map/while/body/eval_jaxpr/dot_general | solution.py:49
  709.6 9.2 %convolution_add_fusion.4 = f32[192,1024]{1,0:T(8,128)S(1)} fusion(f32[512]{0:T(512)S(1)} %select_multiply_fusion.2, s32[1024]{0:T(1024)S(1)} %iota_add_fusion.4, s32[512]{0:T(512)S(1)} %iota_add_fusion.5, f32[192,1024]{1,0:T(8,128)} %get-tuple-element.190, pred[]{:T(512)S(6)} %compare.5, bf16[192,8192]{1,0:T(8,128)(2,1)} %get-tuple-element.199, ...), kind=kOutput, calls=%fused_computation.13.clone.1 | convolution fusion | flops 210108416 | bytes 1777669 | tf_op jit(solution)/shard_map/while/body/eval_jaxpr/dot_general | solution.py:48
  718.8 9.0 %convolution_add_fusion.5 = f32[192,1024]{1,0:T(8,128)} fusion(f32[192,1024]{1,0:T(8,128)S(1)} %convolution_add_fusion.4, f32[512]{0:T(512)S(1)} %select_multiply_fusion.2, s32[1024]{0:T(1024)S(1)} %iota_add_fusion.4, s32[512]{0:T(512)S(1)} %iota_add_fusion.5, bf16[192,8192]{1,0:T(8,128)(2,1)S(1)} %get-tuple-element.200, s32[]{:T(128)S(6)} %select_n.107), kind=kOutput, calls=%fused_computation.12.clone.1 | convolution fusion | flops 210436096 | bytes 1777668 | tf_op jit(solution)/shard_map/while/body/eval_jaxpr/dot_general | solution.py:49
  727.8 2.2 reshape_reshape.3
  (108 shorter events, 33.9 us)
Async XLA Ops:
  1.8 1.2 copy-start.1
  2.1 45.4 %copy-start.6 = (s32[1,1,18,2]{2,3,1,0:T(2,128)S(1)}, s32[1,1,18,2]{2,3,1,0:T(2,128)}, u32[]{:S(2)}) copy-start(s32[1,1,18,2]{2,3,1,0:T(2,128)} %param.8) | copy-start | bytes 436
  2.1 46.1 %copy-start.7 = (s32[1,1,18,1]{2,3,1,0:T(1,128)S(1)}, s32[1,1,18,1]{2,3,1,0:T(1,128)}, u32[]{:S(2)}) copy-start(s32[1,1,18,1]{2,3,1,0:T(1,128)} %param.9) | copy-start | bytes 220
  3.7 14.2 %collective-permute-start = (bf16[16,2,2,8192]{3,0,2,1:T(8,128)(2,1)S(1)}, bf16[16,2,2,8192]{3,0,2,1:T(8,128)(2,1)S(1)}, u32[]{:S(2)}, u32[]{:S(2)}) collective-permute-start(bf16[16,2,2,8192]{3,0,2,1:T(8,128)(2,1)S(1)} %multiply_convert_fusion.5), channel_id=1, source_target_pairs={{0,1},{1,2},{2,3},{3,4},{4,5},{5,6},{6,7},{7,0},{8,9},{9,10},{10,1... | collective-permute-start | bytes 3145736 | tf_op jit(solution)/shard_map/ppermute | solution.py:20
  17.9 14.2 %collective-permute-start.1 = (bf16[16,2,2,8192]{3,0,2,1:T(8,128)(2,1)S(1)}, bf16[16,2,2,8192]{3,0,2,1:T(8,128)(2,1)S(1)}, u32[]{:S(2)}, u32[]{:S(2)}) collective-permute-start(bf16[16,2,2,8192]{3,0,2,1:T(8,128)(2,1)S(1)} %collective-permute-done), channel_id=1, source_target_pairs={{0,1},{1,2},{2,3},{3,4},{4,5},{5,6},{6,7},{7,0},{8,9},{9,10},{10,1... | collective-permute-start | bytes 3145736 | tf_op jit(solution)/shard_map/ppermute | solution.py:20
  17.9 15.2 %collective-permute-start.4 = (bf16[16,2,2,8192]{3,0,2,1:T(8,128)(2,1)S(1)}, bf16[16,2,2,8192]{3,0,2,1:T(8,128)(2,1)}, u32[]{:S(2)}, u32[]{:S(2)}) collective-permute-start(bf16[16,2,2,8192]{3,0,2,1:T(8,128)(2,1)S(1)} %multiply_convert_fusion.5), channel_id=1, source_target_pairs={{0,7},{1,0},{2,1},{3,2},{4,3},{5,4},{6,5},{7,6},{8,15},{9,8},{10,9... | collective-permute-start | bytes 3145736 | tf_op jit(solution)/shard_map/ppermute | solution.py:22
  32.2 1.0 copy-start.4
  33.1 14.3 %collective-permute-start.2 = (bf16[16,2,2,8192]{3,0,2,1:T(8,128)(2,1)S(1)}, bf16[16,2,2,8192]{3,0,2,1:T(8,128)(2,1)}, u32[]{:S(2)}, u32[]{:S(2)}) collective-permute-start(bf16[16,2,2,8192]{3,0,2,1:T(8,128)(2,1)S(1)} %collective-permute-done.1), channel_id=1, source_target_pairs={{0,1},{1,2},{2,3},{3,4},{4,5},{5,6},{6,7},{7,0},{8,9},{9,10},{10,1... | collective-permute-start | bytes 3145736 | tf_op jit(solution)/shard_map/ppermute | solution.py:20
  33.1 15.2 %collective-permute-start.5 = (bf16[16,2,2,8192]{3,0,2,1:T(8,128)(2,1)}, bf16[16,2,2,8192]{3,0,2,1:T(8,128)(2,1)}, u32[]{:S(2)}, u32[]{:S(2)}) collective-permute-start(bf16[16,2,2,8192]{3,0,2,1:T(8,128)(2,1)} %collective-permute-done.4), channel_id=1, source_target_pairs={{0,7},{1,0},{2,1},{3,2},{4,3},{5,4},{6,5},{7,6},{8,15},{9,8},{10,9... | collective-permute-start | bytes 3145736 | tf_op jit(solution)/shard_map/ppermute | solution.py:22
  47.5 14.5 %collective-permute-start.3 = (bf16[16,2,2,8192]{3,0,2,1:T(8,128)(2,1)}, bf16[16,2,2,8192]{3,0,2,1:T(8,128)(2,1)}, u32[]{:S(2)}, u32[]{:S(2)}) collective-permute-start(bf16[16,2,2,8192]{3,0,2,1:T(8,128)(2,1)} %collective-permute-done.2), channel_id=1, source_target_pairs={{0,1},{1,2},{2,3},{3,4},{4,5},{5,6},{6,7},{7,0},{8,9},{9,10},{10,1... | collective-permute-start | bytes 3145736 | tf_op jit(solution)/shard_map/ppermute | solution.py:20
  48.1 18.4 %copy-start.5 = (bf16[16,2,2,8192]{3,0,2,1:T(8,128)(2,1)S(1)}, bf16[16,2,2,8192]{3,0,2,1:T(8,128)(2,1)}, u32[]{:S(2)}) copy-start(bf16[16,2,2,8192]{3,0,2,1:T(8,128)(2,1)} %copy-done.4) | copy-start | bytes 3145732
  48.4 26.2 %collective-permute-start.6 = (bf16[16,2,2,8192]{3,0,2,1:T(8,128)(2,1)}, bf16[16,2,2,8192]{3,0,2,1:T(8,128)(2,1)S(1)}, u32[]{:S(2)}, u32[]{:S(2)}) collective-permute-start(bf16[16,2,2,8192]{3,0,2,1:T(8,128)(2,1)} %collective-permute-done.5), channel_id=1, source_target_pairs={{0,7},{1,0},{2,1},{3,2},{4,3},{5,4},{6,5},{7,6},{8,15},{9,8},{10,9... | collective-permute-start | bytes 3145736 | tf_op jit(solution)/shard_map/ppermute | solution.py:22
  157.6 3.1 copy-start.3
  159.1 2.0 copy-start.2
  162.6 2.2 copy-start
  175.9 107.6 %all-to-all-start = ((bf16[16,3,4,2,8192]{4,3,2,1,0:T(2,128)(2,1)}), bf16[16,3,4,2,8192]{4,3,2,1,0:T(2,128)(2,1)}, u32[]{:S(2)}, u32[]{:S(2)}) async-start(bf16[16,3,4,2,8192]{4,3,2,1,0:T(2,128)(2,1)} %bitcast.52), calls=%async_computation | async-start | bytes 12582912 | tf_op jit(solution)/shard_map/all_to_all | solution.py:101
  283.5 120.8 %all-to-all-start.1 = ((bf16[16,3,4,2,8192]{4,3,2,1,0:T(2,128)(2,1)}), bf16[16,3,4,2,8192]{4,3,2,1,0:T(2,128)(2,1)}, u32[]{:S(2)}, u32[]{:S(2)}) async-start(bf16[16,3,4,2,8192]{4,3,2,1,0:T(2,128)(2,1)} %bitcast.51), calls=%async_computation.1 | async-start | bytes 12582912 | tf_op jit(solution)/shard_map/all_to_all | solution.py:101
